TPU v7x, 256 devices: a whole 4x4x8 slice. The times are simulated.
256 devices in a mesh: row: 64 (over z, x, core), col: 4 (over y).
Axes of the slice: x: 4, y: 4, z: 8, core: 2. Of those that a mesh axis runs over, the one named last changes fastest.
Arguments:
- hamiltonian: bfloat16 [128, 4, 2, 2, 128, 128], P('row', 'col'), may hold values from -0.14142136 to 0.14142136, as said below
- density: float32 [128, 4, 2, 2, 128, 128], P('row', 'col'), may hold values from -6.4 to 6.4, as said below
- block_cols: int32 [128, 4, 2], P('row', 'col'), may hold values from 0 to 127, as said below
Outputs:
- commutator: float32 [128, 4, 2, 2, 128, 128], P('row', 'col')
- density_section: float32 [128, 4, 2, 2, 128, 128], P('row', 'col')
Inputs may be any that keep to these rules, and one draw needn't show every extreme that they name: `block_cols`: block rows 2 d to 2 d + 1 lie on device d along row. A permutation drawn for each device gives each of its block rows a fiber f from 0 to 1, each fiber once a device. With P the number of devices along col and t = (c - d) mod P, slot (c, 0) of a block row of fiber f on device d holds the block row of fiber f on device (d + t) mod (64); slot (c, 1) holds, for t > 0, the block row of fiber f on device (d + t - P) mod (64), and for t = 0 the block row of fiber f + 1 - 2 (f mod 2) on device d. So the pattern is symmetric and every slot (i, j) lies in column group (j div 2) mod P. `hamiltonian`: Hermitian: the block of row i for column j is the conjugate transpose of the block of row j for column i. `density`: Hermitian: the block of row i for column j is the conjugate transpose of the block of row j for column i.
All inputs are finite; a program needn't handle non-finite values.
Results may differ from a plain program's by a relative error of at most 0.0029.
Values may be sent and summed in bfloat16 or wider, within the bound.
A program may use at most 64 MiB of HBM per device.

v0:
```python
import functools

import jax
import jax.numpy as jnp
from jax import lax
from jax.experimental import pallas as pl
from jax.experimental.pallas import tpu as pltpu
from jax.sharding import PartitionSpec as P

MESH = pl.DeviceIdType.MESH


def kernel(
    rows, cols, cols_ref, h_ref, d_ref, comm_ref, sect_ref,
    hbuf, dbuf, stage, acc, pbuf, mbuf,
    hsend, hrecv, dsend, drecv, psend, precv, lsem,
):
    d = lax.axis_index("row")
    c = lax.axis_index("col")
    t = lax.rem(c + rows - d, cols)
    reach = cols - 1
    span = 2 * reach + 1

    def row_at(o):
        return lax.rem(d + o + rows, rows)

    def col_at(j):
        return lax.rem(c + j + cols, cols)

    up, down = col_at(1), col_at(-1)

    swaps = [lax.rem(cols_ref[0, 0, s], 2) == 1 for s in range(2)]

    def pair(s, ref):
        first, second = ref[0], ref[1]
        return (lax.select_n(swaps[s], first, second), lax.select_n(swaps[s], second, first))

    def h_index(tt, s):
        return tt + reach if s == 0 else jnp.where(tt > 0, tt - 1, span)

    def needed(o, s):
        if s == 0:
            return o >= t - reach
        return jnp.where(t > 0, o <= t - 1, o == 0)

    loads = []
    for s in range(2):
        copy = pltpu.make_async_copy(d_ref.at[:, 0, s], stage.at[s], lsem.at[s])
        copy.start()
        loads.append(copy)
    for s in range(2):
        i = h_index(t, s)
        pltpu.make_async_copy(h_ref.at[:, 0, s], hbuf.at[i], hrecv.at[i]).start()

    barrier = pltpu.get_barrier_semaphore()
    for o in range(-reach, reach + 1):
        if o:
            pl.semaphore_signal(barrier, inc=1, device_id=(row_at(o), c), device_id_type=MESH)
    for other in (up, down):
        pl.semaphore_signal(barrier, inc=1, device_id=(d, other), device_id_type=MESH)

    for s in range(2):
        loads[s].wait()
        for r, block in enumerate(pair(s, stage.at[s])):
            dbuf[reach, s, r] = block.astype(jnp.bfloat16)
    acc[...] = jnp.zeros_like(acc)
    pl.semaphore_wait(barrier, 2 * reach + 2)

    def h_copy(s, other, sem, tt):
        i = h_index(tt, s)
        own = h_ref.at[:, 0, s]
        return pltpu.make_async_remote_copy(
            src_ref=own, dst_ref=hbuf.at[i], send_sem=hsend.at[sem], recv_sem=hrecv.at[i],
            device_id=(d, other), device_id_type=MESH,
        )

    def h_relay(s, other, sem, tt):
        i = h_index(tt, s)
        return pltpu.make_async_remote_copy(
            src_ref=hbuf.at[i], dst_ref=hbuf.at[i], send_sem=hsend.at[sem], recv_sem=hrecv.at[i],
            device_id=(d, other), device_id_type=MESH,
        )

    t_down = lax.rem(t + cols - 1, cols)
    t_up = lax.rem(t + 1, cols)
    h_copies = [
        (h_copy(0, up, 0, t), None),
        (h_copy(1, down, 1, t), t > 0),
        (h_copy(1, up, 2, t), t > 0),
        (h_copy(0, down, 3, t), None),
    ]
    relays = [
        (h_relay(0, up, 4, t_down), None),
        (h_relay(1, down, 5, t_up), t_up > 0),
    ]

    def when(cond, f):
        if cond is None:
            f()
        else:
            pl.when(cond)(f)

    for copy, cond in h_copies[:2]:
        when(cond, copy.start)

    d_copies = []
    for o in (1, -1, 2, -2, 3, -3):
        for s in range(2):
            there = jnp.where(jnp.where(s == 0, t, t - cols) - o >= 0, 0, 1)
            copy = pltpu.make_async_remote_copy(
                src_ref=dbuf.at[reach, s], dst_ref=dbuf.at[reach - o, there],
                send_sem=dsend.at[o + reach, s], recv_sem=drecv.at[reach - o, there],
                device_id=(row_at(o), c), device_id_type=MESH,
            )
            if s == 0:
                cond = o >= t - reach
            else:
                cond = jnp.logical_and(t > 0, o <= t - 1)
            d_copies.append((copy, cond))
    for copy, cond in d_copies:
        when(cond, copy.start)
    for copy, cond in h_copies[2:]:
        when(cond, copy.start)

    def h_wait(i):
        pltpu.make_async_copy(hbuf.at[i], hbuf.at[i], hrecv.at[i]).wait()

    for (copy, cond), s, tt in zip(relays, (0, 1), (t_down, t_up)):
        def pass_on(copy=copy, s=s, tt=tt):
            h_wait(h_index(tt, s))
            copy.start()

        when(cond, pass_on)

    def add(h_i, d_i, d_s, s):
        for r, den in enumerate(pair(s, dbuf.at[d_i, d_s])):
            h = hbuf[h_i, r]
            left = jnp.concatenate([h[0], h[1]], axis=1)
            right = jnp.concatenate(
                [
                    jnp.concatenate([den[0], den[1]], axis=1),
                    jnp.concatenate([-den[1], den[0]], axis=1),
                ],
                axis=0,
            )
            acc[s, r] += jnp.dot(left, right, preferred_element_type=jnp.float32)

    for j in (0, reach, 1, 2):
        tt = lax.rem(t + j, cols)
        for half in range(2):
            o = tt if half == 0 else tt - cols

            def step(o=o, half=half, tt=tt, j=j):
                i = o + reach
                if j == 0 or (j, half) not in ((reach, 0), (1, 1)):
                    h_wait(i)
                for s in range(2):
                    def term(s=s):
                        @pl.when(o != 0)
                        def _():
                            pltpu.make_async_copy(
                                dbuf.at[i, s], dbuf.at[i, s], drecv.at[i, s]
                            ).wait()

                        add(i, i, s, s)

                    pl.when(needed(o, s))(term)

            if half == 0:
                step()
            else:
                pl.when(tt > 0)(step)
            if j == 0 and half == 1:
                @pl.when(t == 0)
                def _():
                    h_wait(span)
                    for s in range(2):
                        add(span, reach, 1 - s, s)

    p_copies = []
    home = lax.rem(d, cols)
    for s in range(2):
        p_copies.append(
            pltpu.make_async_remote_copy(
                src_ref=pbuf.at[s], dst_ref=mbuf.at[1 - s],
                send_sem=psend.at[s], recv_sem=precv.at[1 - s],
                device_id=(row_at(t - cols * s), home), device_id_type=MESH,
            )
        )
    for s in range(2):
        pbuf[s] = acc[s].astype(jnp.bfloat16)
    for s in range(2):
        pl.when(t > 0)(p_copies[s].start)
    for s in range(2):
        @pl.when(t == 0)
        def _(s=s):
            mbuf[s] = pbuf[s]

        @pl.when(t > 0)
        def _(s=s):
            pltpu.make_async_copy(mbuf.at[s], mbuf.at[s], precv.at[s]).wait()

    bs = acc.shape[2]
    for s in range(2):
        for r, mirror in enumerate(pair(s, mbuf.at[s])):
            mirror = mirror.astype(jnp.float32)
            real = acc[s, r, :, :bs] - mirror[:, :bs].T
            imag = acc[s, r, :, bs:] + mirror[:, bs:].T
            comm_ref[r, 0, s, 0] = real
            comm_ref[r, 0, s, 1] = imag
            sect_ref[r, 0, s, 0] = stage[s, r, 0] + 0.05 * imag
            sect_ref[r, 0, s, 1] = stage[s, r, 1] - 0.05 * real

    for copy, cond in h_copies + relays + d_copies:
        when(cond, copy.wait_send)
    for copy in p_copies:
        pl.when(t > 0)(copy.wait_send)


def body(hamiltonian, density, block_cols):
    rows, cols = lax.axis_size("row"), lax.axis_size("col")
    bs = density.shape[-1]
    span = 2 * cols - 1
    out = jax.ShapeDtypeStruct(density.shape, jnp.float32)
    half = jnp.bfloat16
    comm, sect = pl.pallas_call(
        functools.partial(kernel, rows, cols),
        out_shape=(out, out),
        in_specs=[
            pl.BlockSpec(memory_space=pltpu.SMEM),
            pl.BlockSpec(memory_space=pl.ANY),
            pl.BlockSpec(memory_space=pl.ANY),
        ],
        out_specs=[pl.BlockSpec(memory_space=pltpu.VMEM)] * 2,
        scratch_shapes=[
            pltpu.VMEM((span + 1, 2, 2, bs, bs), half),
            pltpu.VMEM((span, 2, 2, 2, bs, bs), half),
            pltpu.VMEM((2, 2, 2, bs, bs), jnp.float32),
            pltpu.VMEM((2, 2, bs, 2 * bs), jnp.float32),
            pltpu.VMEM((2, 2, bs, 2 * bs), half),
            pltpu.VMEM((2, 2, bs, 2 * bs), half),
            pltpu.SemaphoreType.DMA((6,)),
            pltpu.SemaphoreType.DMA((span + 1,)),
            pltpu.SemaphoreType.DMA((span, 2)),
            pltpu.SemaphoreType.DMA((span, 2)),
            pltpu.SemaphoreType.DMA((2,)),
            pltpu.SemaphoreType.DMA((2,)),
            pltpu.SemaphoreType.DMA((2,)),
        ],
        compiler_params=pltpu.CompilerParams(collective_id=0, has_side_effects=True),
        name="commutator",
    )(block_cols, hamiltonian, density)
    return comm, sect


def solution(mesh):
    in_specs = (
        P("row", "col", None, None, None, None),
        P("row", "col", None, None, None, None),
        P("row", "col", None),
    )
    out_specs = (P("row", "col", None, None, None, None), P("row", "col", None, None, None, None))
    return jax.shard_map(body, mesh=mesh, in_specs=in_specs, out_specs=out_specs, check_vma=False)
```

profile of v0, /device:TPU:17, one launch (start us, length us, event | category | flops | bytes accessed | tf_op | source)
XLA Modules:
  0.0 36.2 jit_solution(1643377385754590928)
XLA Ops:
  0.6 32.8 %commutator.1 = (f32[2,1,2,2,128,128]{5,4,3,2,1,0:T(8,128)}, f32[2,1,2,2,128,128]{5,4,3,2,1,0:T(8,128)}) custom-call(s32[2,1,2]{2,1,0:T(1,128)} %cols_ref.1, bf16[2,1,2,2,128,128]{5,4,3,2,1,0:T(8,128)(2,1)} %h_ref.1, f32[2,1,2,2,128,128]{5,4,3,2,1,0:T(8,128)} %d_ref.1), custom_call_target="tpu_custom_call" | custom-call | tf_op jit(solution)/shard_map/commutator/pallas_call | solution.py:226
  33.4 0.0 copy-start
  33.5 1.9 %copy.7 = f32[2,1,2,2,128,128]{5,4,3,2,1,0:T(8,128)} copy(f32[2,1,2,2,128,128]{5,4,3,2,1,0:T(8,128)} %get-tuple-element.4) | data formatting | bytes 1048576
  35.4 0.0 copy-done
  35.4 0.8 %copy.8 = f32[2,1,2,2,128,128]{5,4,3,2,1,0:T(8,128)} copy(f32[2,1,2,2,128,128]{5,4,3,2,1,0:T(8,128)S(1)} %copy-done) | data formatting | bytes 1048576
Async XLA Ops:
  33.4 1.9 %copy-start = (f32[2,1,2,2,128,128]{5,4,3,2,1,0:T(8,128)S(1)}, f32[2,1,2,2,128,128]{5,4,3,2,1,0:T(8,128)}, u32[]{:S(2)}) copy-start(f32[2,1,2,2,128,128]{5,4,3,2,1,0:T(8,128)} %get-tuple-element.5) | copy-start | bytes 1572868
where the time goes:
time: 36.3 us; the launch traced here: 36.2 us
  Pallas kernels  32.8 us (90%)
  local copies, waits for them, and re-layouts  2.73 us (8%)
  between operations  0.65 us (2%)
    pallas_call x1, Pallas kernels, body(): pl.pallas_call(functools.partial(kernel, rows, cols), out_shape=(out, out...  32.8 us
    unnamed x4, local copies, waits for them, and re-layouts  2.73 us

commit v1 on v0

v1 whole, which is shorter than its diff:
```python
import functools

import jax
import jax.numpy as jnp
from jax import lax
from jax.experimental import pallas as pl
from jax.experimental.pallas import tpu as pltpu
from jax.sharding import PartitionSpec as P

MESH = pl.DeviceIdType.MESH


def kernel(
    rows, cols, cols_ref, h_ref, d_ref, comm_ref, sect_ref,
    cbuf, hbuf, dbuf, stage, acc, pbuf, mbuf,
    hsend, hrecv, dsend, drecv, psend, precv, lsem,
):
    d = lax.axis_index("row")
    c = lax.axis_index("col")
    t = lax.rem(c + rows - d, cols)
    side = 1 - 2 * lax.rem(d, 2)
    reach = cols - 1
    span = 2 * reach + 1
    place = (t, t - cols)
    valid = (t >= 0, t > 0)
    both = jnp.logical_and

    def row_at(o):
        return lax.rem(d + o + rows, rows)

    up, down = lax.rem(c + 1, cols), lax.rem(c + cols - 1, cols)
    t_down, t_up = lax.rem(t + cols - 1, cols), lax.rem(t + 1, cols)

    def h_index(tt, s):
        return tt + reach if s == 0 else jnp.where(tt > 0, tt - 1, span)

    def needed(o, s):
        if s == 0:
            return o >= t - reach
        return jnp.where(t > 0, o <= t - 1, o == 0)

    cols_load = pltpu.make_async_copy(cols_ref, cbuf, lsem.at[2])
    cols_load.start()
    loads = [pltpu.make_async_copy(d_ref.at[:, 0, s], stage.at[s], lsem.at[s]) for s in range(2)]
    for copy in loads:
        copy.start()
    for s in range(2):
        i = h_index(t, s)
        for r in range(2):
            pltpu.make_async_copy(h_ref.at[r, 0, s], hbuf.at[i, r], hrecv.at[i, r]).start()

    barrier = pltpu.get_barrier_semaphore()
    for o in (side, -side, 3 * side, 2 * side, -2 * side):
        pl.semaphore_signal(barrier, inc=1, device_id=(row_at(o), c), device_id_type=MESH)
    for other in (up, down):
        pl.semaphore_signal(barrier, inc=1, device_id=(d, other), device_id_type=MESH)

    cols_load.wait()
    swaps = [lax.rem(cbuf[0, 0, s], 2) == 1 for s in range(2)]

    def pair(s, ref):
        first, second = ref[0], ref[1]
        return (lax.select_n(swaps[s], first, second), lax.select_n(swaps[s], second, first))

    for s in range(2):
        loads[s].wait()
        for r, block in enumerate(pair(s, stage.at[s])):
            dbuf[reach, s, r] = block.astype(jnp.bfloat16)
    acc[...] = jnp.zeros_like(acc)
    pl.semaphore_wait(barrier, 7)

    def h_copies(s, other, tt, first, own):
        i = h_index(tt, s)
        return [
            pltpu.make_async_remote_copy(
                src_ref=h_ref.at[r, 0, s] if own else hbuf.at[i, r],
                dst_ref=hbuf.at[i, r],
                send_sem=hsend.at[first + r],
                recv_sem=hrecv.at[i, r],
                device_id=(d, other),
                device_id_type=MESH,
            )
            for r in range(2)
        ]

    def h_wait(i, r):
        pltpu.make_async_copy(hbuf.at[i, r], hbuf.at[i, r], hrecv.at[i, r]).wait()

    def unit(o, s, by, sem):
        there = jnp.where(place[s] - by >= 0, 0, 1)
        i = o - by + reach
        return pltpu.make_async_remote_copy(
            src_ref=dbuf.at[o + reach, s],
            dst_ref=dbuf.at[i, there],
            send_sem=dsend.at[sem, s],
            recv_sem=drecv.at[i, there],
            device_id=(row_at(by), c),
            device_id_type=MESH,
        )

    def d_wait(o, s):
        pltpu.make_async_copy(
            dbuf.at[o + reach, s], dbuf.at[o + reach, s], drecv.at[o + reach, s]
        ).wait()

    turn = [side * p for p in place]
    own_far = [(unit(0, s, -side, 0), both(valid[s], turn[s] <= 2)) for s in range(2)]
    own_near = [
        (unit(0, s, jnp.where(turn[s] >= 0, 3 * side, 2 * side), 1), both(valid[s], turn[s] >= -1))
        for s in range(2)
    ]
    own_chip = [(unit(0, s, side, 2), both(valid[s], turn[s] >= -2)) for s in range(2)]
    from_far = [both(valid[s], turn[s] <= 2) for s in range(2)]
    from_near = [both(valid[s], turn[s] >= 0) for s in range(2)]
    far_chip = [(unit(-side, s, side, 3), both(from_far[s], turn[s] >= -2)) for s in range(2)]
    far_near = [(unit(-side, s, 2 * side, 4), both(from_far[s], turn[s] >= -1)) for s in range(2)]
    near_chip = [(unit(3 * side, s, side, 5), from_near[s]) for s in range(2)]

    on_up = [(x, valid[0]) for x in h_copies(0, up, t, 0, True)]
    on_down = [(x, valid[1]) for x in h_copies(1, down, t, 2, True)]
    to_up = [(x, valid[1]) for x in h_copies(1, up, t, 4, True)]
    to_down = [(x, valid[0]) for x in h_copies(0, down, t, 6, True)]
    past_up = [(x, valid[0]) for x in h_copies(0, up, t_down, 8, False)]
    past_down = [(x, t_up > 0) for x in h_copies(1, down, t_up, 10, False)]

    def start(copies):
        for copy, cond in copies:
            pl.when(cond)(copy.start)

    for n in range(2):
        start([on_up[n], on_down[n], own_far[n], own_near[n], own_chip[n]])
    start(to_up + to_down)

    for s in range(2):
        @pl.when(from_far[s])
        def _(s=s):
            d_wait(-side, s)
            start([far_near[s], far_chip[s]])

    for s in range(2):
        @pl.when(from_near[s])
        def _(s=s):
            d_wait(3 * side, s)
            start([near_chip[s]])

    for r in range(2):
        h_wait(h_index(t_down, 0), r)
        start([past_up[r]])

        @pl.when(t_up > 0)
        def _(r=r):
            h_wait(h_index(t_up, 1), r)
            start([past_down[r]])

    def add(h_i, r, d_i, d_s, s):
        h = hbuf[h_i, r]
        den = pair(s, dbuf.at[d_i, d_s])[r]
        left = jnp.concatenate([h[0], h[1]], axis=1)
        right = jnp.concatenate(
            [
                jnp.concatenate([den[0], den[1]], axis=1),
                jnp.concatenate([-den[1], den[0]], axis=1),
            ],
            axis=0,
        )
        acc[s, r] += jnp.dot(left, right, preferred_element_type=jnp.float32)

    def terms(o, rs, waits):
        for s in range(2):
            @pl.when(needed(o, s))
            def _(s=s):
                if waits:
                    late = both(both(o != 0, o != -side), o != 3 * side)
                    pl.when(late)(lambda: d_wait(o, s))
                for r in rs:
                    add(o + reach, r, o + reach, s, s)

    @pl.when(t == 0)
    def _():
        for r in range(2):
            h_wait(span, r)
            for s in range(2):
                add(span, r, reach, 1 - s, s)

    def step(n, carry):
        j = jnp.where(n >= 4, cols - 1, n // 2)
        tt = lax.rem(t + j, cols)
        o = tt - cols * lax.rem(n, 2)
        last = n == 6
        o = jnp.where(last, -3 * side, o)
        active = jnp.where(
            last,
            lax.rem(t + 2 + 3 * side + cols, cols) != 0,
            both(jnp.logical_or(lax.rem(n, 2) == 0, tt > 0), o != -3 * side),
        )

        @pl.when(active)
        def _():
            @pl.when(both(o != t_down, o != t_up - cols))
            def _():
                for r in range(2):
                    h_wait(o + reach, r)

            terms(o, (0, 1), True)

        return carry

    lax.fori_loop(0, 7, step, 0)

    home = lax.rem(d, cols)

    def p_copy(s, r):
        return pltpu.make_async_remote_copy(
            src_ref=pbuf.at[s, r],
            dst_ref=mbuf.at[1 - s, r],
            send_sem=psend.at[s, r],
            recv_sem=precv.at[1 - s, r],
            device_id=(row_at(place[s]), home),
            device_id_type=MESH,
        )

    opposite = lax.rem(t + 2, cols)
    for r in range(2):
        h_wait(opposite + reach, r)
        terms(opposite, (r,), r == 0)

        @pl.when(opposite > 0)
        def _(r=r):
            h_wait(opposite - 1, r)
            terms(opposite - cols, (r,), r == 0)

        for s in range(2):
            pbuf[s, r] = acc[s, r].astype(jnp.bfloat16)
        for s in range(2):
            pl.when(t > 0)(p_copy(s, r).start)

    @pl.when(t == 0)
    def _():
        mbuf[...] = pbuf[...]

    bs = acc.shape[2]
    for s in range(2):
        @pl.when(t > 0)
        def _(s=s):
            for r in range(2):
                pltpu.make_async_copy(mbuf.at[s, r], mbuf.at[s, r], precv.at[s, r]).wait()

        for r, mirror in enumerate(pair(s, mbuf.at[s])):
            mirror = mirror.astype(jnp.float32)
            real = acc[s, r, :, :bs] - mirror[:, :bs].T
            imag = acc[s, r, :, bs:] + mirror[:, bs:].T
            comm_ref[r, 0, s, 0] = real
            comm_ref[r, 0, s, 1] = imag
            sect_ref[r, 0, s, 0] = stage[s, r, 0] + 0.05 * imag
            sect_ref[r, 0, s, 1] = stage[s, r, 1] - 0.05 * real

    for copy, cond in (
        on_up + on_down + to_up + to_down + past_up + past_down
        + own_far + own_near + own_chip + far_chip + far_near + near_chip
    ):
        pl.when(cond)(copy.wait_send)
    for s in range(2):
        for r in range(2):
            pl.when(t > 0)(p_copy(s, r).wait_send)


def store(comm_ref, sect_ref, comm_out, sect_out, sem):
    copies = [
        pltpu.make_async_copy(comm_ref, comm_out, sem.at[0]),
        pltpu.make_async_copy(sect_ref, sect_out, sem.at[1]),
    ]
    for copy in copies:
        copy.start()
    for copy in copies:
        copy.wait()


def body(hamiltonian, density, block_cols):
    rows, cols = lax.axis_size("row"), lax.axis_size("col")
    bs = density.shape[-1]
    span = 2 * cols - 1
    out = jax.ShapeDtypeStruct(density.shape, jnp.float32)
    half = jnp.bfloat16
    vmem = pl.BlockSpec(memory_space=pltpu.VMEM)
    hbm = pl.BlockSpec(memory_space=pltpu.HBM)
    operands = [
        pltpu.with_memory_space_constraint(x, pltpu.HBM)
        for x in (block_cols, hamiltonian, density)
    ]
    results = pl.pallas_call(
        functools.partial(kernel, rows, cols),
        out_shape=(out, out),
        in_specs=[hbm] * 3,
        out_specs=[vmem] * 2,
        scratch_shapes=[
            pltpu.SMEM(block_cols.shape, jnp.int32),
            pltpu.VMEM((span + 1, 2, 2, bs, bs), half),
            pltpu.VMEM((span, 2, 2, 2, bs, bs), half),
            pltpu.VMEM((2, 2, 2, bs, bs), jnp.float32),
            pltpu.VMEM((2, 2, bs, 2 * bs), jnp.float32),
            pltpu.VMEM((2, 2, bs, 2 * bs), half),
            pltpu.VMEM((2, 2, bs, 2 * bs), half),
            pltpu.SemaphoreType.DMA((12,)),
            pltpu.SemaphoreType.DMA((span + 1, 2)),
            pltpu.SemaphoreType.DMA((6, 2)),
            pltpu.SemaphoreType.DMA((span, 2)),
            pltpu.SemaphoreType.DMA((2, 2)),
            pltpu.SemaphoreType.DMA((2, 2)),
            pltpu.SemaphoreType.DMA((3,)),
        ],
        compiler_params=pltpu.CompilerParams(
            collective_id=0, has_side_effects=True, vmem_limit_bytes=8 * 1024 * 1024
        ),
        name="commutator",
    )(*operands)
    return pl.pallas_call(
        store,
        out_shape=(out, out),
        in_specs=[vmem] * 2,
        out_specs=[pl.BlockSpec(memory_space=pl.ANY)] * 2,
        scratch_shapes=[pltpu.SemaphoreType.DMA((2,))],
        compiler_params=pltpu.CompilerParams(vmem_limit_bytes=4 * 1024 * 1024),
        name="store",
    )(*results)


def solution(mesh):
    in_specs = (
        P("row", "col", None, None, None, None),
        P("row", "col", None, None, None, None),
        P("row", "col", None),
    )
    out_specs = (P("row", "col", None, None, None, None), P("row", "col", None, None, None, None))
    return jax.shard_map(body, mesh=mesh, in_specs=in_specs, out_specs=out_specs, check_vma=False)
```

time: 36.3 us -> 30.8 us (0.85)
  the two profiles are of different devices: /device:TPU:17 before, /device:TPU:16 now
where the time goes in v1:
time: 30.8 us; the launch traced here: 30.7 us
  Pallas kernels  30.1 us (98%)
  between operations  0.64 us (2%)
    pallas_call x1, Pallas kernels, body(): pl.pallas_call(functools.partial(kernel, rows, cols), out_shape=(out, out...  29.1 us
    pallas_call x1, Pallas kernels, body(): pl.pallas_call(store, out_shape=(out, out), in_specs=[vmem] * 2, out_spec...  0.99 us

profile of v1, /device:TPU:16, one launch (start us, length us, event | category | flops | bytes accessed | tf_op | source)
XLA Modules:
  0.0 30.7 jit_solution(14417773486555534652)
XLA Ops:
  0.6 29.1 %commutator.1 = (f32[2,1,2,2,128,128]{5,4,3,2,1,0:T(8,128)S(1)}, f32[2,1,2,2,128,128]{5,4,3,2,1,0:T(8,128)S(1)}) custom-call(s32[2,1,2]{2,1,0:T(1,128)} %cols_ref.1, bf16[2,1,2,2,128,128]{5,4,3,2,1,0:T(8,128)(2,1)} %h_ref.1, f32[2,1,2,2,128,128]{5,4,3,2,1,0:T(8,128)} %d_ref.1), custom_call_target="tpu_custom_call" | custom-call | tf_op jit(solution)/shard_map/commutator/pallas_call | solution.py:290
  29.7 1.0 %store.1 = (f32[2,1,2,2,128,128]{5,4,3,2,1,0:T(8,128)}, f32[2,1,2,2,128,128]{5,4,3,2,1,0:T(8,128)}) custom-call(f32[2,1,2,2,128,128]{5,4,3,2,1,0:T(8,128)S(1)} %get-tuple-element.4.comm_ref, f32[2,1,2,2,128,128]{5,4,3,2,1,0:T(8,128)S(1)} %get-tuple-element.5.sect_ref), custom_call_target="tpu_custom_call" | custom-call | tf_op jit(solution)/shard_map/store/pallas_call | solution.py:316

commit v2 on v1

--- a/solution.py
+++ b/solution.py
@@ -62,95 +62,130 @@
         first, second = ref[0], ref[1]
         return (lax.select_n(swaps[s], first, second), lax.select_n(swaps[s], second, first))
 
+    acc[...] = jnp.zeros_like(acc)
+    pl.semaphore_wait(barrier, 7)
+
+    def start(copies):
+        for copy, cond in copies:
+            pl.when(cond)(copy.start)
+
+    def h_copy(s, r, other, tt, sem, own):
+        i = h_index(tt, s)
+        return pltpu.make_async_remote_copy(
+            src_ref=h_ref.at[r, 0, s] if own else hbuf.at[i, r],
+            dst_ref=hbuf.at[i, r],
+            send_sem=hsend.at[sem],
+            recv_sem=hrecv.at[i, r],
+            device_id=(d, other),
+            device_id_type=MESH,
+        )
+
+    def goes_up(s, r, tt):
+        return {(0, 0): tt >= 0, (0, 1): tt >= 2, (1, 1): tt == 3}[s, r]
+
+    def goes_down(s, r, tt):
+        return {(1, 0): tt > 0, (1, 1): both(tt > 0, tt < 3), (0, 1): tt < 2}[s, r]
+
+    def h_wait(i, r):
+        pltpu.make_async_copy(hbuf.at[i, r], hbuf.at[i, r], hrecv.at[i, r]).wait()
+
+    up_order = ((0, 0), (0, 1), (1, 1), (1, 0))
+    down_order = ((1, 0), (1, 1), (0, 1), (0, 0))
+    h_own = []
+    for n in range(4):
+        (s, r), (z, q) = up_order[n], down_order[n]
+        h_own.append((h_copy(s, r, up, t, n, True), valid[s]))
+        h_own.append((h_copy(z, q, down, t, 4 + n, True), valid[z]))
+    start(h_own)
+    h_past = {}
+    for n in range(3):
+        (s, r), (z, q) = up_order[n], down_order[n]
+        h_past["up", s, r] = (h_copy(s, r, up, t_down, 8 + n, False), goes_up(s, r, t_down))
+        h_past["down", z, q] = (h_copy(z, q, down, t_up, 11 + n, False), goes_down(z, q, t_up))
+
+    def h_pass(way, s, r):
+        copy, cond = h_past[way, s, r]
+
+        @pl.when(cond)
+        def _():
+            h_wait(h_index(t_down if way == "up" else t_up, s), r)
+            copy.start()
+
     for s in range(2):
         loads[s].wait()
         for r, block in enumerate(pair(s, stage.at[s])):
             dbuf[reach, s, r] = block.astype(jnp.bfloat16)
-    acc[...] = jnp.zeros_like(acc)
-    pl.semaphore_wait(barrier, 7)
-
-    def h_copies(s, other, tt, first, own):
-        i = h_index(tt, s)
-        return [
-            pltpu.make_async_remote_copy(
-                src_ref=h_ref.at[r, 0, s] if own else hbuf.at[i, r],
-                dst_ref=hbuf.at[i, r],
-                send_sem=hsend.at[first + r],
-                recv_sem=hrecv.at[i, r],
-                device_id=(d, other),
-                device_id_type=MESH,
-            )
-            for r in range(2)
-        ]
-
-    def h_wait(i, r):
-        pltpu.make_async_copy(hbuf.at[i, r], hbuf.at[i, r], hrecv.at[i, r]).wait()
-
-    def unit(o, s, by, sem):
+
+    def unit(o, s, r, by, sem):
         there = jnp.where(place[s] - by >= 0, 0, 1)
         i = o - by + reach
         return pltpu.make_async_remote_copy(
-            src_ref=dbuf.at[o + reach, s],
-            dst_ref=dbuf.at[i, there],
-            send_sem=dsend.at[sem, s],
-            recv_sem=drecv.at[i, there],
+            src_ref=dbuf.at[o + reach, s, r],
+            dst_ref=dbuf.at[i, there, r],
+            send_sem=dsend.at[sem, s, r],
+            recv_sem=drecv.at[i, there, r],
             device_id=(row_at(by), c),
             device_id_type=MESH,
         )
 
-    def d_wait(o, s):
-        pltpu.make_async_copy(
-            dbuf.at[o + reach, s], dbuf.at[o + reach, s], drecv.at[o + reach, s]
-        ).wait()
+    def d_wait(o, s, r):
+        block = dbuf.at[o + reach, s, r]
+        pltpu.make_async_copy(block, block, drecv.at[o + reach, s, r]).wait()
 
     turn = [side * p for p in place]
-    own_far = [(unit(0, s, -side, 0), both(valid[s], turn[s] <= 2)) for s in range(2)]
-    own_near = [
-        (unit(0, s, jnp.where(turn[s] >= 0, 3 * side, 2 * side), 1), both(valid[s], turn[s] >= -1))
-        for s in range(2)
-    ]
-    own_chip = [(unit(0, s, side, 2), both(valid[s], turn[s] >= -2)) for s in range(2)]
     from_far = [both(valid[s], turn[s] <= 2) for s in range(2)]
     from_near = [both(valid[s], turn[s] >= 0) for s in range(2)]
-    far_chip = [(unit(-side, s, side, 3), both(from_far[s], turn[s] >= -2)) for s in range(2)]
-    far_near = [(unit(-side, s, 2 * side, 4), both(from_far[s], turn[s] >= -1)) for s in range(2)]
-    near_chip = [(unit(3 * side, s, side, 5), from_near[s]) for s in range(2)]
-
-    on_up = [(x, valid[0]) for x in h_copies(0, up, t, 0, True)]
-    on_down = [(x, valid[1]) for x in h_copies(1, down, t, 2, True)]
-    to_up = [(x, valid[1]) for x in h_copies(1, up, t, 4, True)]
-    to_down = [(x, valid[0]) for x in h_copies(0, down, t, 6, True)]
-    past_up = [(x, valid[0]) for x in h_copies(0, up, t_down, 8, False)]
-    past_down = [(x, t_up > 0) for x in h_copies(1, down, t_up, 10, False)]
-
-    def start(copies):
-        for copy, cond in copies:
-            pl.when(cond)(copy.start)
-
-    for n in range(2):
-        start([on_up[n], on_down[n], own_far[n], own_near[n], own_chip[n]])
-    start(to_up + to_down)
-
-    for s in range(2):
+    hops = {
+        "far": [(0, -side, from_far[s]) for s in range(2)],
+        "near": [
+            (0, jnp.where(turn[s] >= 0, 3 * side, 2 * side), both(valid[s], turn[s] >= -1))
+            for s in range(2)
+        ],
+        "chip": [(0, side, both(valid[s], turn[s] >= -2)) for s in range(2)],
+        "far near": [(-side, 2 * side, both(from_far[s], turn[s] >= -1)) for s in range(2)],
+        "far chip": [(-side, side, both(from_far[s], turn[s] >= -2)) for s in range(2)],
+        "near chip": [(3 * side, side, from_near[s]) for s in range(2)],
+    }
+    d_copies = {
+        (kind, s, r): (unit(hop[s][0], s, r, hop[s][1], n), hop[s][2])
+        for n, (kind, hop) in enumerate(hops.items())
+        for s in range(2)
+        for r in range(2)
+    }
+    for r in range(2):
+        for s in range(2):
+            start([d_copies[kind, s, r] for kind in ("far", "near", "chip")])
+
+    def d_pass(s, r):
         @pl.when(from_far[s])
-        def _(s=s):
-            d_wait(-side, s)
-            start([far_near[s], far_chip[s]])
-
-    for s in range(2):
+        def _():
+            d_wait(-side, s, r)
+            start([d_copies["far near", s, r], d_copies["far chip", s, r]])
+
         @pl.when(from_near[s])
-        def _(s=s):
-            d_wait(3 * side, s)
-            start([near_chip[s]])
-
-    for r in range(2):
-        h_wait(h_index(t_down, 0), r)
-        start([past_up[r]])
-
-        @pl.when(t_up > 0)
-        def _(r=r):
-            h_wait(h_index(t_up, 1), r)
-            start([past_down[r]])
+        def _():
+            d_wait(3 * side, s, r)
+            start([d_copies["near chip", s, r]])
+
+    for n in range(4):
+        d_pass(n % 2, n // 2)
+        if n < 3:
+            h_pass("up", *up_order[n])
+            h_pass("down", *down_order[n])
+
+    def passed(o, r):
+        if r == 0:
+            return jnp.logical_or(o == t_down, both(o == t_up - cols, t_up > 0))
+        return jnp.logical_or(
+            jnp.logical_or(
+                both(o == t_down, goes_up(0, 1, t_down)),
+                both(o == t_down - cols, goes_up(1, 1, t_down)),
+            ),
+            jnp.logical_or(
+                both(o == t_up - cols, goes_down(1, 1, t_up)),
+                both(o == t_up, goes_down(0, 1, t_up)),
+            ),
+        )
 
     def add(h_i, r, d_i, d_s, s):
         h = hbuf[h_i, r]
@@ -170,8 +205,11 @@
             @pl.when(needed(o, s))
             def _(s=s):
                 if waits:
-                    late = both(both(o != 0, o != -side), o != 3 * side)
-                    pl.when(late)(lambda: d_wait(o, s))
+                    @pl.when(both(both(o != 0, o != -side), o != 3 * side))
+                    def _():
+                        for r in range(2):
+                            d_wait(o, s, r)
+
                 for r in rs:
                     add(o + reach, r, o + reach, s, s)
 
@@ -185,9 +223,8 @@
     def step(n, carry):
         j = jnp.where(n >= 4, cols - 1, n // 2)
         tt = lax.rem(t + j, cols)
-        o = tt - cols * lax.rem(n, 2)
         last = n == 6
-        o = jnp.where(last, -3 * side, o)
+        o = jnp.where(last, -3 * side, tt - cols * lax.rem(n, 2))
         active = jnp.where(
             last,
             lax.rem(t + 2 + 3 * side + cols, cols) != 0,
@@ -196,9 +233,9 @@
 
         @pl.when(active)
         def _():
-            @pl.when(both(o != t_down, o != t_up - cols))
-            def _():
-                for r in range(2):
+            for r in range(2):
+                @pl.when(jnp.logical_not(passed(o, r)))
+                def _(r=r):
                     h_wait(o + reach, r)
 
             terms(o, (0, 1), True)
@@ -254,10 +291,7 @@
             sect_ref[r, 0, s, 0] = stage[s, r, 0] + 0.05 * imag
             sect_ref[r, 0, s, 1] = stage[s, r, 1] - 0.05 * real
 
-    for copy, cond in (
-        on_up + on_down + to_up + to_down + past_up + past_down
-        + own_far + own_near + own_chip + far_chip + far_near + near_chip
-    ):
+    for copy, cond in h_own + list(h_past.values()) + list(d_copies.values()):
         pl.when(cond)(copy.wait_send)
     for s in range(2):
         for r in range(2):
@@ -300,10 +334,10 @@
             pltpu.VMEM((2, 2, bs, 2 * bs), jnp.float32),
             pltpu.VMEM((2, 2, bs, 2 * bs), half),
             pltpu.VMEM((2, 2, bs, 2 * bs), half),
-            pltpu.SemaphoreType.DMA((12,)),
+            pltpu.SemaphoreType.DMA((14,)),
             pltpu.SemaphoreType.DMA((span + 1, 2)),
-            pltpu.SemaphoreType.DMA((6, 2)),
-            pltpu.SemaphoreType.DMA((span, 2)),
+            pltpu.SemaphoreType.DMA((6, 2, 2)),
+            pltpu.SemaphoreType.DMA((span, 2, 2)),
             pltpu.SemaphoreType.DMA((2, 2)),
             pltpu.SemaphoreType.DMA((2, 2)),
             pltpu.SemaphoreType.DMA((3,)),

time: 30.8 us -> 29.8 us (0.968); the launches traced: 30.7 us -> 29.4 us
  Pallas kernels: 30.1 us -> 28.8 us
    pallas_call x1, Pallas kernels: 29.1 us -> 27.8 us  [body(): pl.pallas_call(functools.partial(kernel, rows, cols), out_shape=(out, out...]
where the time goes in v2:
time: 29.8 us; the launch traced here: 29.4 us
  Pallas kernels  28.8 us (97%)
  between operations  0.64 us (2%)
    pallas_call x1, Pallas kernels, body(): pl.pallas_call(functools.partial(kernel, rows, cols), out_shape=(out, out...  27.8 us
    pallas_call x1, Pallas kernels, body(): pl.pallas_call(store, out_shape=(out, out), in_specs=[vmem] * 2, out_spec...  0.99 us

profile of v2, /device:TPU:16, one launch (start us, length us, event | category | flops | bytes accessed | tf_op | source)
XLA Modules:
  0.0 29.4 jit_solution(5157236304667353037)
XLA Ops:
  0.6 27.8 %commutator.1 = (f32[2,1,2,2,128,128]{5,4,3,2,1,0:T(8,128)S(1)}, f32[2,1,2,2,128,128]{5,4,3,2,1,0:T(8,128)S(1)}) custom-call(s32[2,1,2]{2,1,0:T(1,128)} %cols_ref.1, bf16[2,1,2,2,128,128]{5,4,3,2,1,0:T(8,128)(2,1)} %h_ref.1, f32[2,1,2,2,128,128]{5,4,3,2,1,0:T(8,128)} %d_ref.1), custom_call_target="tpu_custom_call" | custom-call | tf_op jit(solution)/shard_map/commutator/pallas_call | solution.py:324
  28.4 1.0 %store.1 = (f32[2,1,2,2,128,128]{5,4,3,2,1,0:T(8,128)}, f32[2,1,2,2,128,128]{5,4,3,2,1,0:T(8,128)}) custom-call(f32[2,1,2,2,128,128]{5,4,3,2,1,0:T(8,128)S(1)} %get-tuple-element.4.comm_ref, f32[2,1,2,2,128,128]{5,4,3,2,1,0:T(8,128)S(1)} %get-tuple-element.5.sect_ref), custom_call_target="tpu_custom_call" | custom-call | tf_op jit(solution)/shard_map/store/pallas_call | solution.py:350

commit v3 on v2

--- a/solution.py
+++ b/solution.py
@@ -12,8 +12,8 @@
 
 def kernel(
     rows, cols, cols_ref, h_ref, d_ref, comm_ref, sect_ref,
-    cbuf, hbuf, dbuf, stage, acc, pbuf, mbuf,
-    hsend, hrecv, dsend, drecv, psend, precv, lsem,
+    cbuf, hbuf, dbuf, stage, acc, pbuf, mbuf, rbuf,
+    hsend, hrecv, dsend, drecv, psend, precv, rsend, rrecv, lsem,
 ):
     d = lax.axis_index("row")
     c = lax.axis_index("col")
@@ -55,14 +55,12 @@
     for other in (up, down):
         pl.semaphore_signal(barrier, inc=1, device_id=(d, other), device_id_type=MESH)
 
-    cols_load.wait()
-    swaps = [lax.rem(cbuf[0, 0, s], 2) == 1 for s in range(2)]
+    swaps = []
 
     def pair(s, ref):
         first, second = ref[0], ref[1]
         return (lax.select_n(swaps[s], first, second), lax.select_n(swaps[s], second, first))
 
-    acc[...] = jnp.zeros_like(acc)
     pl.semaphore_wait(barrier, 7)
 
     def start(copies):
@@ -81,15 +79,15 @@
         )
 
     def goes_up(s, r, tt):
-        return {(0, 0): tt >= 0, (0, 1): tt >= 2, (1, 1): tt == 3}[s, r]
+        return {(0, 0): tt >= 0, (0, 1): tt > 0}[s, r]
 
     def goes_down(s, r, tt):
-        return {(1, 0): tt > 0, (1, 1): both(tt > 0, tt < 3), (0, 1): tt < 2}[s, r]
+        return {(1, 0): tt > 0, (1, 1): tt > 0, (0, 1): tt == 0}[s, r]
 
     def h_wait(i, r):
         pltpu.make_async_copy(hbuf.at[i, r], hbuf.at[i, r], hrecv.at[i, r]).wait()
 
-    up_order = ((0, 0), (0, 1), (1, 1), (1, 0))
+    up_order = ((0, 0), (0, 1), (1, 0), (1, 1))
     down_order = ((1, 0), (1, 1), (0, 1), (0, 0))
     h_own = []
     for n in range(4):
@@ -98,10 +96,12 @@
         h_own.append((h_copy(z, q, down, t, 4 + n, True), valid[z]))
     start(h_own)
     h_past = {}
+    for n in range(2):
+        s, r = up_order[n]
+        h_past["up", s, r] = (h_copy(s, r, up, t_down, 8 + n, False), goes_up(s, r, t_down))
     for n in range(3):
-        (s, r), (z, q) = up_order[n], down_order[n]
-        h_past["up", s, r] = (h_copy(s, r, up, t_down, 8 + n, False), goes_up(s, r, t_down))
-        h_past["down", z, q] = (h_copy(z, q, down, t_up, 11 + n, False), goes_down(z, q, t_up))
+        s, r = down_order[n]
+        h_past["down", s, r] = (h_copy(s, r, down, t_up, 10 + n, False), goes_down(s, r, t_up))
 
     def h_pass(way, s, r):
         copy, cond = h_past[way, s, r]
@@ -111,13 +111,15 @@
             h_wait(h_index(t_down if way == "up" else t_up, s), r)
             copy.start()
 
+    cols_load.wait()
+    swaps += [lax.rem(cbuf[0, 0, s], 2) == 1 for s in range(2)]
     for s in range(2):
         loads[s].wait()
         for r, block in enumerate(pair(s, stage.at[s])):
             dbuf[reach, s, r] = block.astype(jnp.bfloat16)
 
     def unit(o, s, r, by, sem):
-        there = jnp.where(place[s] - by >= 0, 0, 1)
+        there = jnp.where(t - cols * s - by >= 0, 0, 1)
         i = o - by + reach
         return pltpu.make_async_remote_copy(
             src_ref=dbuf.at[o + reach, s, r],
@@ -132,46 +134,64 @@
         block = dbuf.at[o + reach, s, r]
         pltpu.make_async_copy(block, block, drecv.at[o + reach, s, r]).wait()
 
-    turn = [side * p for p in place]
-    from_far = [both(valid[s], turn[s] <= 2) for s in range(2)]
-    from_near = [both(valid[s], turn[s] >= 0) for s in range(2)]
-    hops = {
-        "far": [(0, -side, from_far[s]) for s in range(2)],
-        "near": [
-            (0, jnp.where(turn[s] >= 0, 3 * side, 2 * side), both(valid[s], turn[s] >= -1))
-            for s in range(2)
-        ],
-        "chip": [(0, side, both(valid[s], turn[s] >= -2)) for s in range(2)],
-        "far near": [(-side, 2 * side, both(from_far[s], turn[s] >= -1)) for s in range(2)],
-        "far chip": [(-side, side, both(from_far[s], turn[s] >= -2)) for s in range(2)],
-        "near chip": [(3 * side, side, from_near[s]) for s in range(2)],
-    }
-    d_copies = {
-        (kind, s, r): (unit(hop[s][0], s, r, hop[s][1], n), hop[s][2])
-        for n, (kind, hop) in enumerate(hops.items())
-        for s in range(2)
-        for r in range(2)
-    }
-    for r in range(2):
-        for s in range(2):
-            start([d_copies[kind, s, r] for kind in ("far", "near", "chip")])
-
-    def d_pass(s, r):
-        @pl.when(from_far[s])
+    def hop(kind, s):
+        turn = side * (t - cols * s)
+        held = jnp.logical_or(s == 0, t > 0)
+        return {
+            "far": (0, -side, turn <= 2),
+            "near": (0, jnp.where(turn >= 0, 3 * side, 2 * side), turn >= -1),
+            "chip": (0, side, turn >= -2),
+            "far near": (-side, 2 * side, both(turn <= 2, turn >= -1)),
+            "far chip": (-side, side, both(turn <= 2, turn >= -2)),
+            "near chip": (3 * side, side, turn >= 0),
+        }[kind] + (held,)
+
+    kinds = ("far", "near", "chip", "far near", "far chip", "near chip")
+
+    def d_copy(kind, s, r):
+        o, by, cond, held = hop(kind, s)
+        return (unit(o, s, r, by, kinds.index(kind)), both(cond, held))
+
+    long_far = (1 + side) // 2
+    for s in (long_far, 1 - long_far):
+        for r in range(2):
+            start([d_copy("far", s, r), d_copy("near", 1 - s, r)])
+    for s in range(2):
+        for r in range(2):
+            start([d_copy("chip", s, r)])
+
+    acc[...] = jnp.zeros_like(acc)
+
+    def far_pass(s, r):
+        _, _, cond, held = hop("far", s)
+
+        @pl.when(both(cond, held))
         def _():
             d_wait(-side, s, r)
-            start([d_copies["far near", s, r], d_copies["far chip", s, r]])
-
-        @pl.when(from_near[s])
+            start([d_copy("far near", s, r), d_copy("far chip", s, r)])
+
+    def near_pass(s, r):
+        _, _, cond, held = hop("near chip", s)
+
+        @pl.when(both(cond, held))
         def _():
             d_wait(3 * side, s, r)
-            start([d_copies["near chip", s, r]])
-
-    for n in range(4):
-        d_pass(n % 2, n // 2)
-        if n < 3:
-            h_pass("up", *up_order[n])
-            h_pass("down", *down_order[n])
+            start([d_copy("near chip", s, r)])
+
+    to_near = jnp.where(both(t > 0, jnp.where(side > 0, t == 3, t > 1)), 1, 0)
+    to_chip = jnp.where(both(t > 0, side < 0), 1, 0)
+    far_pass(to_near, 0)
+    near_pass(to_chip, 0)
+    h_pass("up", *up_order[0])
+    h_pass("down", *down_order[0])
+    far_pass(to_near, 1)
+    near_pass(to_chip, 1)
+    h_pass("up", *up_order[1])
+    h_pass("down", *down_order[1])
+    h_pass("down", *down_order[2])
+    for r in range(2):
+        far_pass(1 - to_near, r)
+        near_pass(1 - to_chip, r)
 
     def passed(o, r):
         if r == 0:
@@ -179,12 +199,9 @@
         return jnp.logical_or(
             jnp.logical_or(
                 both(o == t_down, goes_up(0, 1, t_down)),
-                both(o == t_down - cols, goes_up(1, 1, t_down)),
+                both(o == t_up - cols, goes_down(1, 1, t_up)),
             ),
-            jnp.logical_or(
-                both(o == t_up - cols, goes_down(1, 1, t_up)),
-                both(o == t_up, goes_down(0, 1, t_up)),
-            ),
+            both(o == t_up, goes_down(0, 1, t_up)),
         )
 
     def add(h_i, r, d_i, d_s, s):
@@ -245,6 +262,8 @@
     lax.fori_loop(0, 7, step, 0)
 
     home = lax.rem(d, cols)
+    inner = d >= reach
+    half = both(t == cols // 2, inner)
 
     def p_copy(s, r):
         return pltpu.make_async_remote_copy(
@@ -256,6 +275,34 @@
             device_id_type=MESH,
         )
 
+    def p_over(s):
+        return pltpu.make_async_remote_copy(
+            src_ref=pbuf.at[s, 0],
+            dst_ref=rbuf.at[s],
+            send_sem=psend.at[s, 0],
+            recv_sem=rrecv.at[s],
+            device_id=(d, home),
+            device_id_type=MESH,
+        )
+
+    def p_on(s):
+        return pltpu.make_async_remote_copy(
+            src_ref=rbuf.at[s],
+            dst_ref=mbuf.at[1 - s, 0],
+            send_sem=rsend.at[s],
+            recv_sem=precv.at[1 - s, 0],
+            device_id=(row_at(cols // 2 - cols * s), c),
+            device_id_type=MESH,
+        )
+
+    p_copies = [
+        (p_copy(s, r), both(t > 0, jnp.logical_not(half)) if r == 0 else t > 0)
+        for r in range(2)
+        for s in range(2)
+    ]
+    p_overs = [(p_over(s), half) for s in range(2)]
+    p_ons = [(p_on(s), both(t == 0, inner)) for s in range(2)]
+
     opposite = lax.rem(t + 2, cols)
     for r in range(2):
         h_wait(opposite + reach, r)
@@ -268,12 +315,19 @@
 
         for s in range(2):
             pbuf[s, r] = acc[s, r].astype(jnp.bfloat16)
-        for s in range(2):
-            pl.when(t > 0)(p_copy(s, r).start)
+        if r == 0:
+            start(p_overs)
+        start(p_copies[2 * r : 2 * r + 2])
 
     @pl.when(t == 0)
     def _():
         mbuf[...] = pbuf[...]
+
+    @pl.when(both(t == 0, inner))
+    def _():
+        for s in range(2):
+            pltpu.make_async_copy(rbuf.at[s], rbuf.at[s], rrecv.at[s]).wait()
+            p_ons[s][0].start()
 
     bs = acc.shape[2]
     for s in range(2):
@@ -291,11 +345,12 @@
             sect_ref[r, 0, s, 0] = stage[s, r, 0] + 0.05 * imag
             sect_ref[r, 0, s, 1] = stage[s, r, 1] - 0.05 * real
 
-    for copy, cond in h_own + list(h_past.values()) + list(d_copies.values()):
+    for copy, cond in h_own + list(h_past.values()) + [
+        d_copy(kind, s, r) for kind in kinds for s in range(2) for r in range(2)
+    ]:
         pl.when(cond)(copy.wait_send)
-    for s in range(2):
-        for r in range(2):
-            pl.when(t > 0)(p_copy(s, r).wait_send)
+    for copy, cond in p_copies + p_overs + p_ons:
+        pl.when(cond)(copy.wait_send)
 
 
 def store(comm_ref, sect_ref, comm_out, sect_out, sem):
@@ -334,12 +389,15 @@
             pltpu.VMEM((2, 2, bs, 2 * bs), jnp.float32),
             pltpu.VMEM((2, 2, bs, 2 * bs), half),
             pltpu.VMEM((2, 2, bs, 2 * bs), half),
-            pltpu.SemaphoreType.DMA((14,)),
+            pltpu.VMEM((2, bs, 2 * bs), half),
+            pltpu.SemaphoreType.DMA((13,)),
             pltpu.SemaphoreType.DMA((span + 1, 2)),
             pltpu.SemaphoreType.DMA((6, 2, 2)),
             pltpu.SemaphoreType.DMA((span, 2, 2)),
             pltpu.SemaphoreType.DMA((2, 2)),
             pltpu.SemaphoreType.DMA((2, 2)),
+            pltpu.SemaphoreType.DMA((2,)),
+            pltpu.SemaphoreType.DMA((2,)),
             pltpu.SemaphoreType.DMA((3,)),
         ],
         compiler_params=pltpu.CompilerParams(

time: 29.8 us -> 28.9 us (0.970)
  Pallas kernels: 28.8 us -> 28 us
    pallas_call x1, Pallas kernels: 27.8 us -> 27 us  [body(): pl.pallas_call(functools.partial(kernel, rows, cols), out_shape=(out, out...]
where the time goes in v3:
time: 28.9 us; the launch traced here: 28.6 us
  Pallas kernels  28 us (97%)
  between operations  0.64 us (2%)
    pallas_call x1, Pallas kernels, body(): pl.pallas_call(functools.partial(kernel, rows, cols), out_shape=(out, out...  27 us
    pallas_call x1, Pallas kernels, body(): pl.pallas_call(store, out_shape=(out, out), in_specs=[vmem] * 2, out_spec...  0.99 us

profile of v3, /device:TPU:16, one launch (start us, length us, event | category | flops | bytes accessed | tf_op | source)
XLA Modules:
  0.0 28.6 jit_solution(11654816021800598157)
XLA Ops:
  0.6 27.0 %commutator.1 = (f32[2,1,2,2,128,128]{5,4,3,2,1,0:T(8,128)S(1)}, f32[2,1,2,2,128,128]{5,4,3,2,1,0:T(8,128)S(1)}) custom-call(s32[2,1,2]{2,1,0:T(1,128)} %cols_ref.1, bf16[2,1,2,2,128,128]{5,4,3,2,1,0:T(8,128)(2,1)} %h_ref.1, f32[2,1,2,2,128,128]{5,4,3,2,1,0:T(8,128)} %d_ref.1), custom_call_target="tpu_custom_call" | custom-call | tf_op jit(solution)/shard_map/commutator/pallas_call | solution.py:379
  27.7 1.0 %store.1 = (f32[2,1,2,2,128,128]{5,4,3,2,1,0:T(8,128)}, f32[2,1,2,2,128,128]{5,4,3,2,1,0:T(8,128)}) custom-call(f32[2,1,2,2,128,128]{5,4,3,2,1,0:T(8,128)S(1)} %get-tuple-element.4.comm_ref, f32[2,1,2,2,128,128]{5,4,3,2,1,0:T(8,128)S(1)} %get-tuple-element.5.sect_ref), custom_call_target="tpu_custom_call" | custom-call | tf_op jit(solution)/shard_map/store/pallas_call | solution.py:408

commit v4 on v3

--- a/solution.py
+++ b/solution.py
@@ -61,6 +61,13 @@
         first, second = ref[0], ref[1]
         return (lax.select_n(swaps[s], first, second), lax.select_n(swaps[s], second, first))
 
+    cols_load.wait()
+    swaps += [lax.rem(cbuf[0, 0, s], 2) == 1 for s in range(2)]
+    for s in range(2):
+        loads[s].wait()
+        for r, block in enumerate(pair(s, stage.at[s])):
+            dbuf[reach, s, r] = block.astype(jnp.bfloat16)
+
     pl.semaphore_wait(barrier, 7)
 
     def start(copies):
@@ -94,7 +101,6 @@
         (s, r), (z, q) = up_order[n], down_order[n]
         h_own.append((h_copy(s, r, up, t, n, True), valid[s]))
         h_own.append((h_copy(z, q, down, t, 4 + n, True), valid[z]))
-    start(h_own)
     h_past = {}
     for n in range(2):
         s, r = up_order[n]
@@ -110,13 +116,6 @@
         def _():
             h_wait(h_index(t_down if way == "up" else t_up, s), r)
             copy.start()
-
-    cols_load.wait()
-    swaps += [lax.rem(cbuf[0, 0, s], 2) == 1 for s in range(2)]
-    for s in range(2):
-        loads[s].wait()
-        for r, block in enumerate(pair(s, stage.at[s])):
-            dbuf[reach, s, r] = block.astype(jnp.bfloat16)
 
     def unit(o, s, r, by, sem):
         there = jnp.where(t - cols * s - by >= 0, 0, 1)
@@ -160,6 +159,7 @@
         for r in range(2):
             start([d_copy("chip", s, r)])
 
+    start(h_own)
     acc[...] = jnp.zeros_like(acc)
 
     def far_pass(s, r):

time: 28.9 us -> 28.8 us (level)
  no operation moved by 1% of the time
where the time goes in v4:
time: 28.8 us; the launch traced here: 28.5 us
  Pallas kernels  27.9 us (97%)
  between operations  0.64 us (2%)
    pallas_call x1, Pallas kernels, body(): pl.pallas_call(functools.partial(kernel, rows, cols), out_shape=(out, out...  26.9 us
    pallas_call x1, Pallas kernels, body(): pl.pallas_call(store, out_shape=(out, out), in_specs=[vmem] * 2, out_spec...  0.99 us

profile of v4, /device:TPU:16, one launch (start us, length us, event | category | flops | bytes accessed | tf_op | source)
XLA Modules:
  0.0 28.5 jit_solution(5771649062015531518)
XLA Ops:
  0.6 26.9 %commutator.1 = (f32[2,1,2,2,128,128]{5,4,3,2,1,0:T(8,128)S(1)}, f32[2,1,2,2,128,128]{5,4,3,2,1,0:T(8,128)S(1)}) custom-call(s32[2,1,2]{2,1,0:T(1,128)} %cols_ref.1, bf16[2,1,2,2,128,128]{5,4,3,2,1,0:T(8,128)(2,1)} %h_ref.1, f32[2,1,2,2,128,128]{5,4,3,2,1,0:T(8,128)} %d_ref.1), custom_call_target="tpu_custom_call" | custom-call | tf_op jit(solution)/shard_map/commutator/pallas_call | solution.py:379
  27.6 1.0 %store.1 = (f32[2,1,2,2,128,128]{5,4,3,2,1,0:T(8,128)}, f32[2,1,2,2,128,128]{5,4,3,2,1,0:T(8,128)}) custom-call(f32[2,1,2,2,128,128]{5,4,3,2,1,0:T(8,128)S(1)} %get-tuple-element.4.comm_ref, f32[2,1,2,2,128,128]{5,4,3,2,1,0:T(8,128)S(1)} %get-tuple-element.5.sect_ref), custom_call_target="tpu_custom_call" | custom-call | tf_op jit(solution)/shard_map/store/pallas_call | solution.py:408

commit v5 on v4

--- a/solution.py
+++ b/solution.py
@@ -262,7 +262,7 @@
     lax.fori_loop(0, 7, step, 0)
 
     home = lax.rem(d, cols)
-    inner = d >= reach
+    inner = jnp.logical_or(both(d >= reach, d < 8), d >= rows - 8)
     half = both(t == cols // 2, inner)
 
     def p_copy(s, r):

time: 28.8 us -> 28.8 us (level)
  no operation moved by 1% of the time
where the time goes in v5:
time: 28.8 us; the launch traced here: 28.5 us
  Pallas kernels  27.9 us (97%)
  between operations  0.64 us (2%)
    pallas_call x1, Pallas kernels, body(): pl.pallas_call(functools.partial(kernel, rows, cols), out_shape=(out, out...  26.9 us
    pallas_call x1, Pallas kernels, body(): pl.pallas_call(store, out_shape=(out, out), in_specs=[vmem] * 2, out_spec...  0.99 us

profile of v5, /device:TPU:16, one launch (start us, length us, event | category | flops | bytes accessed | tf_op | source)
XLA Modules:
  0.0 28.5 jit_solution(1141711967722036350)
XLA Ops:
  0.6 26.9 %commutator.1 = (f32[2,1,2,2,128,128]{5,4,3,2,1,0:T(8,128)S(1)}, f32[2,1,2,2,128,128]{5,4,3,2,1,0:T(8,128)S(1)}) custom-call(s32[2,1,2]{2,1,0:T(1,128)} %cols_ref.1, bf16[2,1,2,2,128,128]{5,4,3,2,1,0:T(8,128)(2,1)} %h_ref.1, f32[2,1,2,2,128,128]{5,4,3,2,1,0:T(8,128)} %d_ref.1), custom_call_target="tpu_custom_call" | custom-call | tf_op jit(solution)/shard_map/commutator/pallas_call | solution.py:379
  27.6 1.0 %store.1 = (f32[2,1,2,2,128,128]{5,4,3,2,1,0:T(8,128)}, f32[2,1,2,2,128,128]{5,4,3,2,1,0:T(8,128)}) custom-call(f32[2,1,2,2,128,128]{5,4,3,2,1,0:T(8,128)S(1)} %get-tuple-element.4.comm_ref, f32[2,1,2,2,128,128]{5,4,3,2,1,0:T(8,128)S(1)} %get-tuple-element.5.sect_ref), custom_call_target="tpu_custom_call" | custom-call | tf_op jit(solution)/shard_map/store/pallas_call | solution.py:408

commit v6 on v4

--- a/solution.py
+++ b/solution.py
@@ -329,6 +329,11 @@
             pltpu.make_async_copy(rbuf.at[s], rbuf.at[s], rrecv.at[s]).wait()
             p_ons[s][0].start()
 
+    for copy, cond in h_own + list(h_past.values()) + [
+        d_copy(kind, s, r) for kind in kinds for s in range(2) for r in range(2)
+    ]:
+        pl.when(cond)(copy.wait_send)
+
     bs = acc.shape[2]
     for s in range(2):
         @pl.when(t > 0)
@@ -345,10 +350,6 @@
             sect_ref[r, 0, s, 0] = stage[s, r, 0] + 0.05 * imag
             sect_ref[r, 0, s, 1] = stage[s, r, 1] - 0.05 * real
 
-    for copy, cond in h_own + list(h_past.values()) + [
-        d_copy(kind, s, r) for kind in kinds for s in range(2) for r in range(2)
-    ]:
-        pl.when(cond)(copy.wait_send)
     for copy, cond in p_copies + p_overs + p_ons:
         pl.when(cond)(copy.wait_send)
 

time: 28.8 us -> 28.7 us (level)
  no operation moved by 1% of the time
where the time goes in v6:
time: 28.7 us; the launch traced here: 28.5 us
  Pallas kernels  27.9 us (97%)
  between operations  0.64 us (2%)
    pallas_call x1, Pallas kernels, body(): pl.pallas_call(functools.partial(kernel, rows, cols), out_shape=(out, out...  26.9 us
    pallas_call x1, Pallas kernels, body(): pl.pallas_call(store, out_shape=(out, out), in_specs=[vmem] * 2, out_spec...  0.99 us

profile of v6, /device:TPU:16, one launch (start us, length us, event | category | flops | bytes accessed | tf_op | source)
XLA Modules:
  0.0 28.5 jit_solution(12730951730159725741)
XLA Ops:
  0.6 26.9 %commutator.1 = (f32[2,1,2,2,128,128]{5,4,3,2,1,0:T(8,128)S(1)}, f32[2,1,2,2,128,128]{5,4,3,2,1,0:T(8,128)S(1)}) custom-call(s32[2,1,2]{2,1,0:T(1,128)} %cols_ref.1, bf16[2,1,2,2,128,128]{5,4,3,2,1,0:T(8,128)(2,1)} %h_ref.1, f32[2,1,2,2,128,128]{5,4,3,2,1,0:T(8,128)} %d_ref.1), custom_call_target="tpu_custom_call" | custom-call | tf_op jit(solution)/shard_map/commutator/pallas_call | solution.py:380
  27.5 1.0 %store.1 = (f32[2,1,2,2,128,128]{5,4,3,2,1,0:T(8,128)}, f32[2,1,2,2,128,128]{5,4,3,2,1,0:T(8,128)}) custom-call(f32[2,1,2,2,128,128]{5,4,3,2,1,0:T(8,128)S(1)} %get-tuple-element.4.comm_ref, f32[2,1,2,2,128,128]{5,4,3,2,1,0:T(8,128)S(1)} %get-tuple-element.5.sect_ref), custom_call_target="tpu_custom_call" | custom-call | tf_op jit(solution)/shard_map/store/pallas_call | solution.py:409

commit v7 on v6

--- a/solution.py
+++ b/solution.py
@@ -50,7 +50,7 @@
             pltpu.make_async_copy(h_ref.at[r, 0, s], hbuf.at[i, r], hrecv.at[i, r]).start()
 
     barrier = pltpu.get_barrier_semaphore()
-    for o in (side, -side, 3 * side, 2 * side, -2 * side):
+    for o in (3 * side, -2 * side, 2 * side, -side, side):
         pl.semaphore_signal(barrier, inc=1, device_id=(row_at(o), c), device_id_type=MESH)
     for other in (up, down):
         pl.semaphore_signal(barrier, inc=1, device_id=(d, other), device_id_type=MESH)

time: 28.7 us -> 28.7 us (level)
  no operation moved by 1% of the time
where the time goes in v7:
time: 28.7 us; the launch traced here: 28.4 us
  Pallas kernels  27.8 us (97%)
  between operations  0.64 us (2%)
    pallas_call x1, Pallas kernels, body(): pl.pallas_call(functools.partial(kernel, rows, cols), out_shape=(out, out...  26.8 us
    pallas_call x1, Pallas kernels, body(): pl.pallas_call(store, out_shape=(out, out), in_specs=[vmem] * 2, out_spec...  0.99 us

profile of v7, /device:TPU:16, one launch (start us, length us, event | category | flops | bytes accessed | tf_op | source)
XLA Modules:
  0.0 28.4 jit_solution(8331729444903682113)
XLA Ops:
  0.6 26.8 %commutator.1 = (f32[2,1,2,2,128,128]{5,4,3,2,1,0:T(8,128)S(1)}, f32[2,1,2,2,128,128]{5,4,3,2,1,0:T(8,128)S(1)}) custom-call(s32[2,1,2]{2,1,0:T(1,128)} %cols_ref.1, bf16[2,1,2,2,128,128]{5,4,3,2,1,0:T(8,128)(2,1)} %h_ref.1, f32[2,1,2,2,128,128]{5,4,3,2,1,0:T(8,128)} %d_ref.1), custom_call_target="tpu_custom_call" | custom-call | tf_op jit(solution)/shard_map/commutator/pallas_call | solution.py:380
  27.5 1.0 %store.1 = (f32[2,1,2,2,128,128]{5,4,3,2,1,0:T(8,128)}, f32[2,1,2,2,128,128]{5,4,3,2,1,0:T(8,128)}) custom-call(f32[2,1,2,2,128,128]{5,4,3,2,1,0:T(8,128)S(1)} %get-tuple-element.4.comm_ref, f32[2,1,2,2,128,128]{5,4,3,2,1,0:T(8,128)S(1)} %get-tuple-element.5.sect_ref), custom_call_target="tpu_custom_call" | custom-call | tf_op jit(solution)/shard_map/store/pallas_call | solution.py:409

commit v8 on v7

--- a/solution.py
+++ b/solution.py
@@ -341,6 +341,10 @@
             for r in range(2):
                 pltpu.make_async_copy(mbuf.at[s, r], mbuf.at[s, r], precv.at[s, r]).wait()
 
+        if s == 1:
+            for copy, cond in p_copies + p_overs + p_ons:
+                pl.when(cond)(copy.wait_send)
+
         for r, mirror in enumerate(pair(s, mbuf.at[s])):
             mirror = mirror.astype(jnp.float32)
             real = acc[s, r, :, :bs] - mirror[:, :bs].T
@@ -349,9 +353,6 @@
             comm_ref[r, 0, s, 1] = imag
             sect_ref[r, 0, s, 0] = stage[s, r, 0] + 0.05 * imag
             sect_ref[r, 0, s, 1] = stage[s, r, 1] - 0.05 * real
-
-    for copy, cond in p_copies + p_overs + p_ons:
-        pl.when(cond)(copy.wait_send)
 
 
 def store(comm_ref, sect_ref, comm_out, sect_out, sem):

time: 28.7 us -> 28.7 us (level)
  no operation moved by 1% of the time
where the time goes in v8:
time: 28.7 us; the launch traced here: 28.4 us
  Pallas kernels  27.8 us (97%)
  between operations  0.64 us (2%)
    pallas_call x1, Pallas kernels, body(): pl.pallas_call(functools.partial(kernel, rows, cols), out_shape=(out, out...  26.8 us
    pallas_call x1, Pallas kernels, body(): pl.pallas_call(store, out_shape=(out, out), in_specs=[vmem] * 2, out_spec...  0.99 us

profile of v8, /device:TPU:16, one launch (start us, length us, event | category | flops | bytes accessed | tf_op | source)
XLA Modules:
  0.0 28.4 jit_solution(16440968230599467486)
XLA Ops:
  0.6 26.8 %commutator.1 = (f32[2,1,2,2,128,128]{5,4,3,2,1,0:T(8,128)S(1)}, f32[2,1,2,2,128,128]{5,4,3,2,1,0:T(8,128)S(1)}) custom-call(s32[2,1,2]{2,1,0:T(1,128)} %cols_ref.1, bf16[2,1,2,2,128,128]{5,4,3,2,1,0:T(8,128)(2,1)} %h_ref.1, f32[2,1,2,2,128,128]{5,4,3,2,1,0:T(8,128)} %d_ref.1), custom_call_target="tpu_custom_call" | custom-call | tf_op jit(solution)/shard_map/commutator/pallas_call | solution.py:381
  27.5 1.0 %store.1 = (f32[2,1,2,2,128,128]{5,4,3,2,1,0:T(8,128)}, f32[2,1,2,2,128,128]{5,4,3,2,1,0:T(8,128)}) custom-call(f32[2,1,2,2,128,128]{5,4,3,2,1,0:T(8,128)S(1)} %get-tuple-element.4.comm_ref, f32[2,1,2,2,128,128]{5,4,3,2,1,0:T(8,128)S(1)} %get-tuple-element.5.sect_ref), custom_call_target="tpu_custom_call" | custom-call | tf_op jit(solution)/shard_map/store/pallas_call | solution.py:410
